TPU v7x, 32 devices: a whole 2x2x4 slice. The times are simulated.
32 devices in a mesh: basin: 8 (over y, x, core), tile: 4 (over z).
Axes of the slice: x: 2, y: 2, z: 4, core: 2. Of those that a mesh axis runs over, the one named last changes fastest.
Arguments:
- tile_water: float32 [8, 64, 4096], P('basin', None, 'tile'), may hold values from 0.1 to 3
- tile_frac: float32 [8, 64, 4096], P('basin', None, 'tile'), may hold values from 0.01 to 0.12
- tile_cell: int32 [8, 64, 4096], P('basin', None, 'tile'), may hold values from 0 to 255
- storage: float32 [8, 64, 256], P('basin', 'tile'), may hold values from 0 to 2
- kappa: float32 [8, 64, 256], P('basin', 'tile'), may hold values from 0.4 to 1
- inverse: float32 [8, 64, 256, 256], P('basin', 'tile'), may hold values from -0.25 to 1.15
- cell_mask: int32 [8, 64, 256], P('basin', 'tile'), may hold values 0 or 1
- upstream: int32 [8, 64], P('basin', 'tile'), may hold values from 0 to 15, as said below
Outputs:
- level: float32 [8, 64, 256], P('basin', 'tile')
- discharge: float32 [8, 64, 256], P('basin', 'tile')
Inputs may be any that keep to these rules, and one draw needn't show every extreme that they name: `upstream`: for each reach position and each group of 16 consecutive chains, the values form a permutation of 0 to 15.
All inputs are finite; a program needn't handle non-finite values. No bound on the sum of `cell_mask` on one device may be relied on, other than what follows from the above.
Results may differ from a plain program's by a relative error of at most 0.0001.
Values sent between devices are 32-bit elements; how exact they have to be, the bound alone decides.
A program may use at most 64 MiB of HBM per device.

v0:
```python
import math

import jax
import jax.numpy as jnp
from jax import lax
from jax.sharding import PartitionSpec as P

SUBSTEPS = 3


time_step = 0.5


def passed_along(value, axis, steps):
    count = lax.axis_size(axis)
    initial, last = (max(0, -steps), min(count, count - steps))
    return lax.ppermute(value, axis, [(source, source + steps) for source in range(initial, last)])


def local(tile_water, tile_frac, tile_cell, storage, kappa, inverse, cell_mask, upstream):
    product = tile_frac[0] * tile_water[0]
    cells = tile_cell[0]
    rows = storage.shape[1]
    width = storage.shape[2]
    tiles = product.shape[1]
    cell_ids = jnp.arange(width, dtype=jnp.int32)
    count = lax.axis_size("tile") * rows
    values = product
    owners = cells
    group = math.gcd(count, 4)
    values = values.reshape(count // group, group, tiles)
    owners = owners.reshape(count // group, group, tiles)

    def one_group(items):
        vals, owns = items
        table = (owns[:, :, None] == cell_ids[None, None, :]).astype(jnp.float32)
        return jnp.einsum("ct,ctj->cj", vals, table, precision=lax.Precision.HIGHEST)

    summed = lax.map(one_group, (values, owners))
    runoff = lax.psum_scatter(summed.reshape(count, width), "tile", scatter_dimension=0, tiled=True)
    forcing = time_step * runoff
    mask = cell_mask[0].astype(jnp.float32)
    rates = kappa[0]
    matrices = inverse[0]
    links = upstream[0]
    level = storage[0]
    count = lax.axis_size("basin")
    selector = (links[:, None] == jnp.arange(rows, dtype=jnp.int32)[None, :]).astype(jnp.float32)

    def update(current, inflow):
        vector = current + forcing + inflow
        wet = mask * jnp.einsum("cjk,ck->cj", matrices, vector, precision=lax.Precision.HIGHEST)
        outflow = rates * wet
        return (wet - outflow, outflow)

    def pass_down(outflow):
        received = passed_along(outflow, "basin", 1)
        return jnp.dot(selector, received, precision=lax.Precision.HIGHEST)

    empty = jnp.zeros((rows, width), jnp.float32)
    position = lax.axis_index("basin")

    def front(turn, carry):
        current, outflow_kept, inflow = carry
        section = turn - position
        active = (section >= 0) & (section < SUBSTEPS)
        new_level, outflow = update(current, inflow)
        current = jnp.where(active, new_level, current)
        outflow_kept = jnp.where(active, outflow, outflow_kept)
        return (current, outflow_kept, pass_down(outflow))

    level, discharge, _ = lax.fori_loop(0, count + SUBSTEPS - 1, front, (level, empty, empty))
    return (level[None], discharge[None])


def solution(mesh):
    placed = (
        P("basin", None, "tile"),
        P("basin", None, "tile"),
        P("basin", None, "tile"),
        P("basin", "tile", None),
        P("basin", "tile", None),
        P("basin", "tile", None, None),
        P("basin", "tile", None),
        P("basin", "tile"),
    )
    return jax.shard_map(
        local,
        mesh=mesh,
        in_specs=placed,
        out_specs=(P("basin", "tile", None), P("basin", "tile", None)),
        check_vma=False,
    )
```

profile of v0, /device:TPU:4, one launch (start us, length us, event | category | flops | bytes accessed | tf_op | source)
XLA Modules:
  0.0 184.1 jit_solution(8932831697303135263)
XLA Ops:
  9.5 26.3 %while.29 = (s32[]{:T(128)}, f32[16,4,256]{2,1,0:T(4,128)S(1)}, f32[16,4,1024]{2,1,0:T(4,128)S(1)}, s32[16,4,1024]{2,1,0:T(4,128)S(1)}, s32[]{:T(128)}) while((s32[]{:T(128)}, f32[16,4,256]{2,1,0:T(4,128)S(1)}, f32[16,4,1024]{2,1,0:T(4,128)S(1)}, s32[16,4,1024]{2,1,0:T(4,128)S(1)}, s32[]{:T(128)}) %tuple.55), condition=%wide.region_1.2_spmd.clone, body=%wide.region_0.1_spmd.clone.sunk | while | flops 13631490 | bytes 110665 | solution.py:39
  36.4 20.6 %reduce-scatter.2.cloned.1.call-done = f32[16,256]{1,0:T(8,128)} async-done(((f32[64,256]{1,0:T(8,128)}), f32[16,256]{1,0:T(8,128)}) %reduce-scatter.2.cloned.1.call-update) | async-done | bytes 16400 | tf_op jit(solution)/shard_map/reduce_scatter | solution.py:40
  57.8 118.8 %while.30 = (s32[]{:T(128)}, f32[16,256]{1,0:T(8,128)S(1)}, f32[16,256]{1,0:T(8,128)S(1)}, f32[16,256]{1,0:T(8,128)S(1)}, s32[]{:T(128)}, /*index=5*/f32[16,256]...) while((s32[]{:T(128)}, f32[16,256]{1,0:T(8,128)S(1)}, ...), condition=%wide.region_4.5_spmd.clone, body=%wide.region_3.4_spmd.clone.sunk | while | flops 13406727 | bytes 4571410 | solution.py:72
  57.8 5.7 %fusion.28 = f32[16,1,256]{2,1,0:T(1,128)S(1)} fusion(f32[16,256,256]{2,1,0:T(8,128)} %get-tuple-element.415, f32[16,256,1]{1,0,2:T(8,128)S(1)} %add_bitcast_fusion.2), kind=kOutput, calls=%fused_computation.11.clone.1 | convolution fusion | flops 12582912 | bytes 4227072 | tf_op jit(solution)/shard_map/while/body/eval_jaxpr/cjk,ck->cj/dot_general | solution.py:52
  63.5 1.9 %collective-permute-start = (f32[16,256]{1,0:T(8,128)S(1)}, f32[16,256]{1,0:T(8,128)S(1)}, u32[]{:S(2)}, u32[]{:S(2)}) collective-permute-start(f32[16,256]{1,0:T(8,128)S(1)} %get-tuple-element.366), channel_id=1, source_target_pairs={{0,4},{4,8},{8,12},{12,16},{16,20},{20,24},{24,28},{1,5},{5,9},{9,... | collective-permute-start | bytes 49160 | tf_op jit(solution)/shard_map/while/body/eval_jaxpr/ppermute | solution.py:17
  65.5 4.0 %collective-permute-done = f32[16,256]{1,0:T(8,128)S(1)} collective-permute-done((f32[16,256]{1,0:T(8,128)S(1)}, f32[16,256]{1,0:T(8,128)S(1)}, u32[]{:S(2)}, u32[]{:S(2)}) %collective-permute-start) | collective-permute-done | bytes 16416 | tf_op jit(solution)/shard_map/while/body/eval_jaxpr/ppermute | solution.py:17
  69.7 5.7 %fusion.28 = f32[16,1,256]{2,1,0:T(1,128)S(1)} fusion(f32[16,256,256]{2,1,0:T(8,128)} %get-tuple-element.415, f32[16,256,1]{1,0,2:T(8,128)S(1)} %add_bitcast_fusion.2), kind=kOutput, calls=%fused_computation.11.clone.1 | convolution fusion | flops 12582912 | bytes 4227072 | tf_op jit(solution)/shard_map/while/body/eval_jaxpr/cjk,ck->cj/dot_general | solution.py:52
  75.4 1.9 %collective-permute-start = (f32[16,256]{1,0:T(8,128)S(1)}, f32[16,256]{1,0:T(8,128)S(1)}, u32[]{:S(2)}, u32[]{:S(2)}) collective-permute-start(f32[16,256]{1,0:T(8,128)S(1)} %get-tuple-element.366), channel_id=1, source_target_pairs={{0,4},{4,8},{8,12},{12,16},{16,20},{20,24},{24,28},{1,5},{5,9},{9,... | collective-permute-start | bytes 49160 | tf_op jit(solution)/shard_map/while/body/eval_jaxpr/ppermute | solution.py:17
  77.4 4.0 %collective-permute-done = f32[16,256]{1,0:T(8,128)S(1)} collective-permute-done((f32[16,256]{1,0:T(8,128)S(1)}, f32[16,256]{1,0:T(8,128)S(1)}, u32[]{:S(2)}, u32[]{:S(2)}) %collective-permute-start) | collective-permute-done | bytes 16416 | tf_op jit(solution)/shard_map/while/body/eval_jaxpr/ppermute | solution.py:17
  81.6 5.7 %fusion.28 = f32[16,1,256]{2,1,0:T(1,128)S(1)} fusion(f32[16,256,256]{2,1,0:T(8,128)} %get-tuple-element.415, f32[16,256,1]{1,0,2:T(8,128)S(1)} %add_bitcast_fusion.2), kind=kOutput, calls=%fused_computation.11.clone.1 | convolution fusion | flops 12582912 | bytes 4227072 | tf_op jit(solution)/shard_map/while/body/eval_jaxpr/cjk,ck->cj/dot_general | solution.py:52
  87.3 1.9 %collective-permute-start = (f32[16,256]{1,0:T(8,128)S(1)}, f32[16,256]{1,0:T(8,128)S(1)}, u32[]{:S(2)}, u32[]{:S(2)}) collective-permute-start(f32[16,256]{1,0:T(8,128)S(1)} %get-tuple-element.366), channel_id=1, source_target_pairs={{0,4},{4,8},{8,12},{12,16},{16,20},{20,24},{24,28},{1,5},{5,9},{9,... | collective-permute-start | bytes 49160 | tf_op jit(solution)/shard_map/while/body/eval_jaxpr/ppermute | solution.py:17
  89.2 4.0 %collective-permute-done = f32[16,256]{1,0:T(8,128)S(1)} collective-permute-done((f32[16,256]{1,0:T(8,128)S(1)}, f32[16,256]{1,0:T(8,128)S(1)}, u32[]{:S(2)}, u32[]{:S(2)}) %collective-permute-start) | collective-permute-done | bytes 16416 | tf_op jit(solution)/shard_map/while/body/eval_jaxpr/ppermute | solution.py:17
  93.5 5.7 %fusion.28 = f32[16,1,256]{2,1,0:T(1,128)S(1)} fusion(f32[16,256,256]{2,1,0:T(8,128)} %get-tuple-element.415, f32[16,256,1]{1,0,2:T(8,128)S(1)} %add_bitcast_fusion.2), kind=kOutput, calls=%fused_computation.11.clone.1 | convolution fusion | flops 12582912 | bytes 4227072 | tf_op jit(solution)/shard_map/while/body/eval_jaxpr/cjk,ck->cj/dot_general | solution.py:52
  99.2 1.9 %collective-permute-start = (f32[16,256]{1,0:T(8,128)S(1)}, f32[16,256]{1,0:T(8,128)S(1)}, u32[]{:S(2)}, u32[]{:S(2)}) collective-permute-start(f32[16,256]{1,0:T(8,128)S(1)} %get-tuple-element.366), channel_id=1, source_target_pairs={{0,4},{4,8},{8,12},{12,16},{16,20},{20,24},{24,28},{1,5},{5,9},{9,... | collective-permute-start | bytes 49160 | tf_op jit(solution)/shard_map/while/body/eval_jaxpr/ppermute | solution.py:17
  101.1 4.0 %collective-permute-done = f32[16,256]{1,0:T(8,128)S(1)} collective-permute-done((f32[16,256]{1,0:T(8,128)S(1)}, f32[16,256]{1,0:T(8,128)S(1)}, u32[]{:S(2)}, u32[]{:S(2)}) %collective-permute-start) | collective-permute-done | bytes 16416 | tf_op jit(solution)/shard_map/while/body/eval_jaxpr/ppermute | solution.py:17
  105.4 5.7 %fusion.28 = f32[16,1,256]{2,1,0:T(1,128)S(1)} fusion(f32[16,256,256]{2,1,0:T(8,128)} %get-tuple-element.415, f32[16,256,1]{1,0,2:T(8,128)S(1)} %add_bitcast_fusion.2), kind=kOutput, calls=%fused_computation.11.clone.1 | convolution fusion | flops 12582912 | bytes 4227072 | tf_op jit(solution)/shard_map/while/body/eval_jaxpr/cjk,ck->cj/dot_general | solution.py:52
  111.1 1.9 %collective-permute-start = (f32[16,256]{1,0:T(8,128)S(1)}, f32[16,256]{1,0:T(8,128)S(1)}, u32[]{:S(2)}, u32[]{:S(2)}) collective-permute-start(f32[16,256]{1,0:T(8,128)S(1)} %get-tuple-element.366), channel_id=1, source_target_pairs={{0,4},{4,8},{8,12},{12,16},{16,20},{20,24},{24,28},{1,5},{5,9},{9,... | collective-permute-start | bytes 49160 | tf_op jit(solution)/shard_map/while/body/eval_jaxpr/ppermute | solution.py:17
  113.0 4.0 %collective-permute-done = f32[16,256]{1,0:T(8,128)S(1)} collective-permute-done((f32[16,256]{1,0:T(8,128)S(1)}, f32[16,256]{1,0:T(8,128)S(1)}, u32[]{:S(2)}, u32[]{:S(2)}) %collective-permute-start) | collective-permute-done | bytes 16416 | tf_op jit(solution)/shard_map/while/body/eval_jaxpr/ppermute | solution.py:17
  117.3 5.7 %fusion.28 = f32[16,1,256]{2,1,0:T(1,128)S(1)} fusion(f32[16,256,256]{2,1,0:T(8,128)} %get-tuple-element.415, f32[16,256,1]{1,0,2:T(8,128)S(1)} %add_bitcast_fusion.2), kind=kOutput, calls=%fused_computation.11.clone.1 | convolution fusion | flops 12582912 | bytes 4227072 | tf_op jit(solution)/shard_map/while/body/eval_jaxpr/cjk,ck->cj/dot_general | solution.py:52
  122.9 1.9 %collective-permute-start = (f32[16,256]{1,0:T(8,128)S(1)}, f32[16,256]{1,0:T(8,128)S(1)}, u32[]{:S(2)}, u32[]{:S(2)}) collective-permute-start(f32[16,256]{1,0:T(8,128)S(1)} %get-tuple-element.366), channel_id=1, source_target_pairs={{0,4},{4,8},{8,12},{12,16},{16,20},{20,24},{24,28},{1,5},{5,9},{9,... | collective-permute-start | bytes 49160 | tf_op jit(solution)/shard_map/while/body/eval_jaxpr/ppermute | solution.py:17
  124.9 4.0 %collective-permute-done = f32[16,256]{1,0:T(8,128)S(1)} collective-permute-done((f32[16,256]{1,0:T(8,128)S(1)}, f32[16,256]{1,0:T(8,128)S(1)}, u32[]{:S(2)}, u32[]{:S(2)}) %collective-permute-start) | collective-permute-done | bytes 16416 | tf_op jit(solution)/shard_map/while/body/eval_jaxpr/ppermute | solution.py:17
  129.1 5.7 %fusion.28 = f32[16,1,256]{2,1,0:T(1,128)S(1)} fusion(f32[16,256,256]{2,1,0:T(8,128)} %get-tuple-element.415, f32[16,256,1]{1,0,2:T(8,128)S(1)} %add_bitcast_fusion.2), kind=kOutput, calls=%fused_computation.11.clone.1 | convolution fusion | flops 12582912 | bytes 4227072 | tf_op jit(solution)/shard_map/while/body/eval_jaxpr/cjk,ck->cj/dot_general | solution.py:52
  134.8 1.9 %collective-permute-start = (f32[16,256]{1,0:T(8,128)S(1)}, f32[16,256]{1,0:T(8,128)S(1)}, u32[]{:S(2)}, u32[]{:S(2)}) collective-permute-start(f32[16,256]{1,0:T(8,128)S(1)} %get-tuple-element.366), channel_id=1, source_target_pairs={{0,4},{4,8},{8,12},{12,16},{16,20},{20,24},{24,28},{1,5},{5,9},{9,... | collective-permute-start | bytes 49160 | tf_op jit(solution)/shard_map/while/body/eval_jaxpr/ppermute | solution.py:17
  136.8 4.0 %collective-permute-done = f32[16,256]{1,0:T(8,128)S(1)} collective-permute-done((f32[16,256]{1,0:T(8,128)S(1)}, f32[16,256]{1,0:T(8,128)S(1)}, u32[]{:S(2)}, u32[]{:S(2)}) %collective-permute-start) | collective-permute-done | bytes 16416 | tf_op jit(solution)/shard_map/while/body/eval_jaxpr/ppermute | solution.py:17
  141.0 5.7 %fusion.28 = f32[16,1,256]{2,1,0:T(1,128)S(1)} fusion(f32[16,256,256]{2,1,0:T(8,128)} %get-tuple-element.415, f32[16,256,1]{1,0,2:T(8,128)S(1)} %add_bitcast_fusion.2), kind=kOutput, calls=%fused_computation.11.clone.1 | convolution fusion | flops 12582912 | bytes 4227072 | tf_op jit(solution)/shard_map/while/body/eval_jaxpr/cjk,ck->cj/dot_general | solution.py:52
  146.7 1.9 %collective-permute-start = (f32[16,256]{1,0:T(8,128)S(1)}, f32[16,256]{1,0:T(8,128)S(1)}, u32[]{:S(2)}, u32[]{:S(2)}) collective-permute-start(f32[16,256]{1,0:T(8,128)S(1)} %get-tuple-element.366), channel_id=1, source_target_pairs={{0,4},{4,8},{8,12},{12,16},{16,20},{20,24},{24,28},{1,5},{5,9},{9,... | collective-permute-start | bytes 49160 | tf_op jit(solution)/shard_map/while/body/eval_jaxpr/ppermute | solution.py:17
  148.7 4.0 %collective-permute-done = f32[16,256]{1,0:T(8,128)S(1)} collective-permute-done((f32[16,256]{1,0:T(8,128)S(1)}, f32[16,256]{1,0:T(8,128)S(1)}, u32[]{:S(2)}, u32[]{:S(2)}) %collective-permute-start) | collective-permute-done | bytes 16416 | tf_op jit(solution)/shard_map/while/body/eval_jaxpr/ppermute | solution.py:17
  152.9 5.7 %fusion.28 = f32[16,1,256]{2,1,0:T(1,128)S(1)} fusion(f32[16,256,256]{2,1,0:T(8,128)} %get-tuple-element.415, f32[16,256,1]{1,0,2:T(8,128)S(1)} %add_bitcast_fusion.2), kind=kOutput, calls=%fused_computation.11.clone.1 | convolution fusion | flops 12582912 | bytes 4227072 | tf_op jit(solution)/shard_map/while/body/eval_jaxpr/cjk,ck->cj/dot_general | solution.py:52
  158.6 1.9 %collective-permute-start = (f32[16,256]{1,0:T(8,128)S(1)}, f32[16,256]{1,0:T(8,128)S(1)}, u32[]{:S(2)}, u32[]{:S(2)}) collective-permute-start(f32[16,256]{1,0:T(8,128)S(1)} %get-tuple-element.366), channel_id=1, source_target_pairs={{0,4},{4,8},{8,12},{12,16},{16,20},{20,24},{24,28},{1,5},{5,9},{9,... | collective-permute-start | bytes 49160 | tf_op jit(solution)/shard_map/while/body/eval_jaxpr/ppermute | solution.py:17
  160.5 4.0 %collective-permute-done = f32[16,256]{1,0:T(8,128)S(1)} collective-permute-done((f32[16,256]{1,0:T(8,128)S(1)}, f32[16,256]{1,0:T(8,128)S(1)}, u32[]{:S(2)}, u32[]{:S(2)}) %collective-permute-start) | collective-permute-done | bytes 16416 | tf_op jit(solution)/shard_map/while/body/eval_jaxpr/ppermute | solution.py:17
  164.8 5.7 %fusion.28 = f32[16,1,256]{2,1,0:T(1,128)S(1)} fusion(f32[16,256,256]{2,1,0:T(8,128)} %get-tuple-element.415, f32[16,256,1]{1,0,2:T(8,128)S(1)} %add_bitcast_fusion.2), kind=kOutput, calls=%fused_computation.11.clone.1 | convolution fusion | flops 12582912 | bytes 4227072 | tf_op jit(solution)/shard_map/while/body/eval_jaxpr/cjk,ck->cj/dot_general | solution.py:52
  172.4 4.0 %collective-permute-done = f32[16,256]{1,0:T(8,128)S(1)} collective-permute-done((f32[16,256]{1,0:T(8,128)S(1)}, f32[16,256]{1,0:T(8,128)S(1)}, u32[]{:S(2)}, u32[]{:S(2)}) %collective-permute-start) | collective-permute-done | bytes 16416 | tf_op jit(solution)/shard_map/while/body/eval_jaxpr/ppermute | solution.py:17
  (128 shorter events, 34.6 us)
Async XLA Ops:
  7.2 49.9 %reduce-scatter.2.cloned.1.call-start = ((), (), s32[]{:S(2)}) async-start(), calls=%async_computation.1 | async-start | bytes 81920 | tf_op jit(solution)/shard_map/reduce_scatter | solution.py:40
  7.2 29.2 %copy-start.4 = (s32[1,16,256]{2,1,0:T(8,128)S(1)}, s32[1,16,256]{2,1,0:T(8,128)}, u32[]{:S(2)}) copy-start(s32[1,16,256]{2,1,0:T(8,128)} %param.18) | copy-start | bytes 49156
  7.2 50.6 %copy-start.1 = (f32[1,16,256]{2,1,0:T(8,128)S(1)}, f32[1,16,256]{2,1,0:T(8,128)}, u32[]{:S(2)}) copy-start(f32[1,16,256]{2,1,0:T(8,128)} %param.15) | copy-start | bytes 49156
  7.2 50.5 %copy-start.2 = (f32[1,16,256]{2,1,0:T(8,128)S(1)}, f32[1,16,256]{2,1,0:T(8,128)}, u32[]{:S(2)}) copy-start(f32[1,16,256]{2,1,0:T(8,128)} %param.16) | copy-start | bytes 49156
  7.3 50.5 %copy-start.5 = (s32[1,16]{1,0:T(1,128)S(1)}, s32[1,16]{1,0:T(1,128)}, u32[]{:S(2)}) copy-start(s32[1,16]{1,0:T(1,128)} %param.19) | copy-start | bytes 196
  63.5 6.0 %collective-permute-start = (f32[16,256]{1,0:T(8,128)S(1)}, f32[16,256]{1,0:T(8,128)S(1)}, u32[]{:S(2)}, u32[]{:S(2)}) collective-permute-start(f32[16,256]{1,0:T(8,128)S(1)} %get-tuple-element.366), channel_id=1, source_target_pairs={{0,4},{4,8},{8,12},{12,16},{16,20},{20,24},{24,28},{1,5},{5,9},{9,... | collective-permute-start | bytes 49160 | tf_op jit(solution)/shard_map/while/body/eval_jaxpr/ppermute | solution.py:17
  75.4 6.0 %collective-permute-start = (f32[16,256]{1,0:T(8,128)S(1)}, f32[16,256]{1,0:T(8,128)S(1)}, u32[]{:S(2)}, u32[]{:S(2)}) collective-permute-start(f32[16,256]{1,0:T(8,128)S(1)} %get-tuple-element.366), channel_id=1, source_target_pairs={{0,4},{4,8},{8,12},{12,16},{16,20},{20,24},{24,28},{1,5},{5,9},{9,... | collective-permute-start | bytes 49160 | tf_op jit(solution)/shard_map/while/body/eval_jaxpr/ppermute | solution.py:17
  87.3 6.0 %collective-permute-start = (f32[16,256]{1,0:T(8,128)S(1)}, f32[16,256]{1,0:T(8,128)S(1)}, u32[]{:S(2)}, u32[]{:S(2)}) collective-permute-start(f32[16,256]{1,0:T(8,128)S(1)} %get-tuple-element.366), channel_id=1, source_target_pairs={{0,4},{4,8},{8,12},{12,16},{16,20},{20,24},{24,28},{1,5},{5,9},{9,... | collective-permute-start | bytes 49160 | tf_op jit(solution)/shard_map/while/body/eval_jaxpr/ppermute | solution.py:17
  99.2 6.0 %collective-permute-start = (f32[16,256]{1,0:T(8,128)S(1)}, f32[16,256]{1,0:T(8,128)S(1)}, u32[]{:S(2)}, u32[]{:S(2)}) collective-permute-start(f32[16,256]{1,0:T(8,128)S(1)} %get-tuple-element.366), channel_id=1, source_target_pairs={{0,4},{4,8},{8,12},{12,16},{16,20},{20,24},{24,28},{1,5},{5,9},{9,... | collective-permute-start | bytes 49160 | tf_op jit(solution)/shard_map/while/body/eval_jaxpr/ppermute | solution.py:17
  111.1 6.0 %collective-permute-start = (f32[16,256]{1,0:T(8,128)S(1)}, f32[16,256]{1,0:T(8,128)S(1)}, u32[]{:S(2)}, u32[]{:S(2)}) collective-permute-start(f32[16,256]{1,0:T(8,128)S(1)} %get-tuple-element.366), channel_id=1, source_target_pairs={{0,4},{4,8},{8,12},{12,16},{16,20},{20,24},{24,28},{1,5},{5,9},{9,... | collective-permute-start | bytes 49160 | tf_op jit(solution)/shard_map/while/body/eval_jaxpr/ppermute | solution.py:17
  122.9 6.0 %collective-permute-start = (f32[16,256]{1,0:T(8,128)S(1)}, f32[16,256]{1,0:T(8,128)S(1)}, u32[]{:S(2)}, u32[]{:S(2)}) collective-permute-start(f32[16,256]{1,0:T(8,128)S(1)} %get-tuple-element.366), channel_id=1, source_target_pairs={{0,4},{4,8},{8,12},{12,16},{16,20},{20,24},{24,28},{1,5},{5,9},{9,... | collective-permute-start | bytes 49160 | tf_op jit(solution)/shard_map/while/body/eval_jaxpr/ppermute | solution.py:17
  134.8 6.0 %collective-permute-start = (f32[16,256]{1,0:T(8,128)S(1)}, f32[16,256]{1,0:T(8,128)S(1)}, u32[]{:S(2)}, u32[]{:S(2)}) collective-permute-start(f32[16,256]{1,0:T(8,128)S(1)} %get-tuple-element.366), channel_id=1, source_target_pairs={{0,4},{4,8},{8,12},{12,16},{16,20},{20,24},{24,28},{1,5},{5,9},{9,... | collective-permute-start | bytes 49160 | tf_op jit(solution)/shard_map/while/body/eval_jaxpr/ppermute | solution.py:17
  146.7 6.0 %collective-permute-start = (f32[16,256]{1,0:T(8,128)S(1)}, f32[16,256]{1,0:T(8,128)S(1)}, u32[]{:S(2)}, u32[]{:S(2)}) collective-permute-start(f32[16,256]{1,0:T(8,128)S(1)} %get-tuple-element.366), channel_id=1, source_target_pairs={{0,4},{4,8},{8,12},{12,16},{16,20},{20,24},{24,28},{1,5},{5,9},{9,... | collective-permute-start | bytes 49160 | tf_op jit(solution)/shard_map/while/body/eval_jaxpr/ppermute | solution.py:17
  158.6 6.0 %collective-permute-start = (f32[16,256]{1,0:T(8,128)S(1)}, f32[16,256]{1,0:T(8,128)S(1)}, u32[]{:S(2)}, u32[]{:S(2)}) collective-permute-start(f32[16,256]{1,0:T(8,128)S(1)} %get-tuple-element.366), channel_id=1, source_target_pairs={{0,4},{4,8},{8,12},{12,16},{16,20},{20,24},{24,28},{1,5},{5,9},{9,... | collective-permute-start | bytes 49160 | tf_op jit(solution)/shard_map/while/body/eval_jaxpr/ppermute | solution.py:17
  170.5 6.0 %collective-permute-start = (f32[16,256]{1,0:T(8,128)S(1)}, f32[16,256]{1,0:T(8,128)S(1)}, u32[]{:S(2)}, u32[]{:S(2)}) collective-permute-start(f32[16,256]{1,0:T(8,128)S(1)} %get-tuple-element.366), channel_id=1, source_target_pairs={{0,4},{4,8},{8,12},{12,16},{16,20},{20,24},{24,28},{1,5},{5,9},{9,... | collective-permute-start | bytes 49160 | tf_op jit(solution)/shard_map/while/body/eval_jaxpr/ppermute | solution.py:17
  176.6 0.6 copy-start
  176.7 0.6 copy-start.3
Sparse Core Ops, SparseCore 0:
  36.5 20.4 reduce-scatter.1
where the time goes:
time: 185 us; the launch traced here: 184 us
  matrix products  84.3 us (46%)
  waiting for transfers between devices  60.7 us (33%)
  starting transfers between devices  19.2 us (10%)
  between operations  14.1 us (8%)
  local copies, waits for them, and re-layouts  2.66 us (1%)
  other arithmetic  2.19 us (1%)
    dot_general x10, matrix products, update(): jnp.einsum('cjk,ck->cj', matrices, vector, precision=lax.Precision.HIGHEST)  56.6 us
    ppermute x10, waiting for transfers between devices, passed_along(): lax.ppermute(value, axis, [(source, source + steps) for source in range(i...  40.1 us
    dot_general x16, matrix products, one_group(): jnp.einsum('ct,ctj->cj', vals, table, precision=lax.Precision.HIGHEST)  25.8 us
    reduce_scatter x1, waiting for transfers between devices, local(): lax.psum_scatter(summed.reshape(count, width), 'tile', scatter_dimension=...  20.6 us
    ppermute x10, starting transfers between devices, passed_along(): lax.ppermute(value, axis, [(source, source + steps) for source in range(i...  19.2 us
  transfers between devices with their start and end apart: 11, of which 11 were waited for; matrix products, arithmetic and copies ran while one was open for 0% of the time, Pallas kernels for 0%

commit v1 on v0

v1 whole, which is shorter than its diff:
```python
import functools

import jax
import jax.numpy as jnp
from jax import lax
from jax.experimental import pallas as pl
from jax.experimental.pallas import tpu as pltpu
from jax.sharding import PartitionSpec as P

SUBSTEPS = 3
time_step = 0.5
MESH = pl.DeviceIdType.MESH
NT = (((1,), (1,)), ((), ()))


def two_terms(value):
    head = value.astype(jnp.bfloat16)
    return head, (value - head.astype(jnp.float32)).astype(jnp.bfloat16)


def iota(shape, axis):
    return lax.broadcasted_iota(jnp.int32, shape, axis)


def kernel(npos, nset, water_hbm, frac_hbm, cell_hbm, storage_ref, kappa_ref, inverse_hbm, mask_ref, upstream_ref,
           level_ref, discharge_ref,
           water, frac, cell, inverse, heads, tails, part, arrived, flow, inflow,
           tile_sem, inverse_sem, part_send, part_recv, flow_send, flow_recv):
    rows, width = storage_ref.shape[1], storage_ref.shape[2]
    low = 1 << (width.bit_length() // 2)
    high = width // low
    here = lax.axis_index("basin")
    mine = lax.axis_index("tile")

    barrier = pltpu.get_barrier_semaphore()
    for step in range(1, nset):
        pl.semaphore_signal(barrier, inc=1, device_id={"tile": lax.rem(mine + step, nset)}, device_id_type=MESH)

    @pl.when(here > 0)
    def _():
        pl.semaphore_signal(barrier, inc=1, device_id={"basin": here - 1}, device_id_type=MESH)

    @pl.when(here < npos - 1)
    def _():
        pl.semaphore_signal(barrier, inc=1, device_id={"basin": here + 1}, device_id_type=MESH)

    steps = list(range(1, nset)) + [0]
    loads = []
    for order, step in enumerate(steps):
        owner = lax.rem(mine + step, nset)
        where = pl.ds(pl.multiple_of(owner * rows, rows), rows)
        group = []
        for at, (source, target) in enumerate(((cell_hbm, cell), (water_hbm, water), (frac_hbm, frac))):
            copy = pltpu.make_async_copy(source.at[0, where], target.at[order], tile_sem.at[order, at])
            copy.start()
            group.append(copy)
        loads.append(group)
    matrix_loads = []
    for chain in range(rows):
        copy = pltpu.make_async_copy(inverse_hbm.at[0, chain], inverse.at[chain], inverse_sem.at[chain])
        copy.start()
        matrix_loads.append(copy)

    same = lax.rem(iota((high * rows, low * rows), 0), rows) == lax.rem(iota((high * rows, low * rows), 1), rows)
    spread = (iota((low * rows, width), 0) // rows == lax.rem(iota((low * rows, width), 1), low)).astype(jnp.bfloat16)
    block = iota((rows, width), 1) // low

    def cell_sums(order):
        cells = cell[order]
        upper = (cells // low).astype(jnp.float32).astype(jnp.bfloat16)
        lower = lax.rem(cells, low).astype(jnp.float32).astype(jnp.bfloat16)
        head, tail = two_terms(frac[order] * water[order])
        zero = jnp.zeros_like(head)
        one = jnp.ones_like(head)
        picks = [upper == jnp.bfloat16(at) for at in range(high)]
        left = jnp.concatenate([jnp.where(pick, head, zero) for pick in picks] + [jnp.where(pick, tail, zero) for pick in picks], axis=0)
        right = jnp.concatenate([jnp.where(lower == jnp.bfloat16(at), one, zero) for at in range(low)], axis=0)
        both = lax.dot_general(left, right, NT, preferred_element_type=jnp.float32)
        crossed = jnp.where(same, both[: high * rows] + both[high * rows:], 0.0)
        head, tail = two_terms(crossed)
        packed = jnp.dot(jnp.concatenate([head, tail], axis=0), spread, preferred_element_type=jnp.float32)
        packed = packed[: high * rows] + packed[high * rows:]
        total = packed[:rows]
        for at in range(1, high):
            total = jnp.where(block == at, packed[at * rows:(at + 1) * rows], total)
        return total

    sends = []
    own = None
    for order, step in enumerate(steps):
        for copy in loads[order]:
            copy.wait()
        sums = cell_sums(order)
        if step == 0:
            own = sums
            continue
        part[step - 1] = sums
        if order == 0:
            pl.semaphore_wait(barrier, nset - 1 + jnp.minimum(here, 1) + jnp.minimum(npos - 1 - here, 1))
        copy = pltpu.make_async_remote_copy(
            src_ref=part.at[step - 1], dst_ref=arrived.at[step - 1],
            send_sem=part_send.at[step - 1], recv_sem=part_recv.at[step - 1],
            device_id={"tile": lax.rem(mine + step, nset)}, device_id_type=MESH)
        copy.start()
        sends.append(copy)

    for chain in range(rows):
        matrix_loads[chain].wait()
        head, tail = two_terms(inverse[chain])
        heads[chain] = head
        tails[chain] = tail

    row = iota((rows, width), 0)
    links = jnp.zeros((rows, width), jnp.int32)
    for chain in range(rows):
        links = jnp.where(row == chain, upstream_ref[0, chain], links)
    live = mask_ref[0].astype(jnp.float32)
    rates = kappa_ref[0]
    picked = [row == chain for chain in range(rows)]

    runoff = own
    for at, copy in enumerate(sends):
        copy.wait_recv()
        runoff = runoff + arrived[at]
    forcing = time_step * runoff

    def product(vector):
        head, tail = two_terms(vector)
        total = jnp.zeros((2 * rows, width), jnp.float32)
        zero = jnp.zeros_like(head)
        for chain in range(rows):
            upper = jnp.where(picked[chain], head, zero)
            left = jnp.concatenate([upper, jnp.where(picked[chain], tail, zero)], axis=0)
            total += lax.dot_general(left, heads[chain], NT, preferred_element_type=jnp.float32)
            total += lax.dot_general(left, tails[chain], NT, preferred_element_type=jnp.float32)
        return total[:rows] + total[rows:]

    @pl.when(here == 0)
    def _():
        inflow[...] = jnp.zeros_like(inflow)

    level = storage_ref[0]
    outflow = level
    for substep in range(SUBSTEPS):
        copy = pltpu.make_async_remote_copy(
            src_ref=flow.at[substep], dst_ref=inflow.at[substep],
            send_sem=flow_send.at[substep], recv_sem=flow_recv.at[substep],
            device_id={"basin": lax.rem(here + 1, npos)}, device_id_type=MESH)

        @pl.when(here > 0)
        def _():
            copy.wait_recv()

        came = inflow[substep]
        incoming = jnp.broadcast_to(came[:1], (rows, width))
        for chain in range(1, rows):
            incoming = jnp.where(links == chain, jnp.broadcast_to(came[chain:chain + 1], (rows, width)), incoming)
        wet = live * product(level + forcing + incoming)
        outflow = rates * wet
        level = wet - outflow

        @pl.when(here < npos - 1)
        def _():
            flow[substep] = outflow
            copy.start()

    level_ref[0] = level
    discharge_ref[0] = outflow

    for copy in sends:
        copy.wait_send()

    @pl.when(here < npos - 1)
    def _():
        for substep in range(SUBSTEPS):
            pltpu.make_async_remote_copy(
                src_ref=flow.at[substep], dst_ref=inflow.at[substep],
                send_sem=flow_send.at[substep], recv_sem=flow_recv.at[substep],
                device_id={"basin": lax.rem(here + 1, npos)}, device_id_type=MESH).wait_send()


def solution(mesh):
    npos, nset = mesh.shape["basin"], mesh.shape["tile"]

    def local(tile_water, tile_frac, tile_cell, storage, kappa, inverse, cell_mask, upstream):
        rows, width = storage.shape[1:]
        tiles = tile_water.shape[2]
        anywhere = pl.BlockSpec(memory_space=pl.ANY)
        vmem = pl.BlockSpec(memory_space=pltpu.VMEM)
        smem = pl.BlockSpec(memory_space=pltpu.SMEM)
        out = jax.ShapeDtypeStruct(storage.shape, jnp.float32)
        return pl.pallas_call(
            functools.partial(kernel, npos, nset),
            out_shape=(out, out),
            in_specs=[anywhere, anywhere, anywhere, vmem, vmem, anywhere, vmem, smem],
            out_specs=(vmem, vmem),
            scratch_shapes=[
                pltpu.VMEM((nset, rows, tiles), jnp.float32),
                pltpu.VMEM((nset, rows, tiles), jnp.float32),
                pltpu.VMEM((nset, rows, tiles), jnp.int32),
                pltpu.VMEM((rows, width, width), jnp.float32),
                pltpu.VMEM((rows, width, width), jnp.bfloat16),
                pltpu.VMEM((rows, width, width), jnp.bfloat16),
                pltpu.VMEM((nset - 1, rows, width), jnp.float32),
                pltpu.VMEM((nset - 1, rows, width), jnp.float32),
                pltpu.VMEM((SUBSTEPS, rows, width), jnp.float32),
                pltpu.VMEM((SUBSTEPS, rows, width), jnp.float32),
                pltpu.SemaphoreType.DMA((nset, 3)),
                pltpu.SemaphoreType.DMA((rows,)),
                pltpu.SemaphoreType.DMA((nset - 1,)),
                pltpu.SemaphoreType.DMA((nset - 1,)),
                pltpu.SemaphoreType.DMA((SUBSTEPS,)),
                pltpu.SemaphoreType.DMA((SUBSTEPS,)),
            ],
            compiler_params=pltpu.CompilerParams(collective_id=0, has_side_effects=True),
        )(tile_water, tile_frac, tile_cell, storage, kappa, inverse, cell_mask, upstream)

    tiled = P("basin", None, "tile")
    chain = P("basin", "tile", None)
    return jax.shard_map(
        local,
        mesh=mesh,
        in_specs=(tiled, tiled, tiled, chain, chain, P("basin", "tile", None, None), chain, P("basin", "tile")),
        out_specs=(chain, chain),
        check_vma=False,
    )
```

time: 185 us -> 46.8 us (0.25)
  the two profiles are of different devices: /device:TPU:4 before, /device:TPU:7 now
where the time goes in v1:
time: 46.8 us; the launch traced here: 46.4 us
  Pallas kernels  43.1 us (92%)
  local copies, waits for them, and re-layouts  2.65 us (6%)
  between operations  0.64 us (1%)
    pallas_call x1, Pallas kernels, local(): pl.pallas_call(functools.partial(kernel, npos, nset), out_shape=(out, out...  43.1 us
    unnamed x2, local copies, waits for them, and re-layouts  2.65 us

profile of v1, /device:TPU:7, one launch (start us, length us, event | category | flops | bytes accessed | tf_op | source)
XLA Modules:
  0.0 46.4 jit_solution(17220224942720697204)
XLA Ops:
  0.6 43.1 %shard_map.95 = (f32[1,16,256]{2,1,0:T(8,128)}, f32[1,16,256]{2,1,0:T(8,128)}) custom-call(f32[1,64,1024]{2,1,0:T(8,128)} %water_hbm.1, f32[1,64,1024]{2,1,0:T(8,128)} %frac_hbm.1, s32[1,64,1024]{2,1,0:T(8,128)} %cell_hbm.1, f32[1,16,256]{2,1,0:T(8,128)} %storage_ref.1, f32[1,16,256]{2,1,0:T(8,128)} %kappa_ref.1, f32[1,16,256,256]{3,2,1,0:T(8,128)} %inverse_hbm.1, ...), custom_call_target="tpu_custom_call" | custom-call | tf_op jit(solution)/shard_map/pallas_call | solution.py:192
  43.7 1.3 %copy.12 = f32[1,16,256]{2,1,0:T(8,128)} copy(f32[1,16,256]{2,1,0:T(8,128)} %get-tuple-element.4) | data formatting | bytes 32768
  45.0 1.3 %copy.13 = f32[1,16,256]{2,1,0:T(8,128)} copy(f32[1,16,256]{2,1,0:T(8,128)} %get-tuple-element.5) | data formatting | bytes 32768

commit v2 on v1

--- a/solution.py
+++ b/solution.py
@@ -23,7 +23,7 @@
 
 
 def kernel(npos, nset, water_hbm, frac_hbm, cell_hbm, storage_ref, kappa_ref, inverse_hbm, mask_ref, upstream_ref,
-           level_ref, discharge_ref,
+           out_ref,
            water, frac, cell, inverse, heads, tails, part, arrived, flow, inflow,
            tile_sem, inverse_sem, part_send, part_recv, flow_send, flow_recv):
     rows, width = storage_ref.shape[1], storage_ref.shape[2]
@@ -106,7 +106,7 @@
 
     for chain in range(rows):
         matrix_loads[chain].wait()
-        head, tail = two_terms(inverse[chain])
+        head, tail = two_terms(inverse[chain].T)
         heads[chain] = head
         tails[chain] = tail
 
@@ -131,8 +131,8 @@
         for chain in range(rows):
             upper = jnp.where(picked[chain], head, zero)
             left = jnp.concatenate([upper, jnp.where(picked[chain], tail, zero)], axis=0)
-            total += lax.dot_general(left, heads[chain], NT, preferred_element_type=jnp.float32)
-            total += lax.dot_general(left, tails[chain], NT, preferred_element_type=jnp.float32)
+            total += jnp.dot(left, heads[chain], preferred_element_type=jnp.float32)
+            total += jnp.dot(left, tails[chain], preferred_element_type=jnp.float32)
         return total[:rows] + total[rows:]
 
     @pl.when(here == 0)
@@ -164,8 +164,8 @@
             flow[substep] = outflow
             copy.start()
 
-    level_ref[0] = level
-    discharge_ref[0] = outflow
+    out_ref[0] = level
+    out_ref[1] = outflow
 
     for copy in sends:
         copy.wait_send()
@@ -188,12 +188,11 @@
         anywhere = pl.BlockSpec(memory_space=pl.ANY)
         vmem = pl.BlockSpec(memory_space=pltpu.VMEM)
         smem = pl.BlockSpec(memory_space=pltpu.SMEM)
-        out = jax.ShapeDtypeStruct(storage.shape, jnp.float32)
-        return pl.pallas_call(
+        out = pl.pallas_call(
             functools.partial(kernel, npos, nset),
-            out_shape=(out, out),
+            out_shape=jax.ShapeDtypeStruct((2, rows, width), jnp.float32),
             in_specs=[anywhere, anywhere, anywhere, vmem, vmem, anywhere, vmem, smem],
-            out_specs=(vmem, vmem),
+            out_specs=vmem,
             scratch_shapes=[
                 pltpu.VMEM((nset, rows, tiles), jnp.float32),
                 pltpu.VMEM((nset, rows, tiles), jnp.float32),
@@ -214,6 +213,7 @@
             ],
             compiler_params=pltpu.CompilerParams(collective_id=0, has_side_effects=True),
         )(tile_water, tile_frac, tile_cell, storage, kappa, inverse, cell_mask, upstream)
+        return out[:1], out[1:]
 
     tiled = P("basin", None, "tile")
     chain = P("basin", "tile", None)

time: 46.8 us -> 35.1 us (0.75)
  Pallas kernels: 43.1 us -> 32.8 us
  local copies, waits for them, and re-layouts: 2.65 us -> 1.35 us
    pallas_call x1, Pallas kernels: 43.1 us -> 32.8 us  [local(): pl.pallas_call(functools.partial(kernel, npos, nset), out_shape=jax.Shape...]
    unnamed x2 -> x0, local copies, waits for them, and re-layouts: 2.65 us -> none
    slice x0 -> x1, local copies, waits for them, and re-layouts: none -> 1.35 us  [local(): return (out[:1], out[1:])]
where the time goes in v2:
time: 35.1 us; the launch traced here: 34.8 us
  Pallas kernels  32.8 us (93%)
  local copies, waits for them, and re-layouts  1.35 us (4%)
  between operations  0.64 us (2%)
    pallas_call x1, Pallas kernels, local(): pl.pallas_call(functools.partial(kernel, npos, nset), out_shape=jax.Shape...  32.8 us
    slice x1, local copies, waits for them, and re-layouts, local(): return (out[:1], out[1:])  1.35 us

profile of v2, /device:TPU:7, one launch (start us, length us, event | category | flops | bytes accessed | tf_op | source)
XLA Modules:
  0.0 34.8 jit_solution(3998630215667757367)
XLA Ops:
  0.6 32.8 %shard_map.95 = f32[2,16,256]{2,1,0:T(8,128)} custom-call(f32[1,64,1024]{2,1,0:T(8,128)} %water_hbm.1, f32[1,64,1024]{2,1,0:T(8,128)} %frac_hbm.1, s32[1,64,1024]{2,1,0:T(8,128)} %cell_hbm.1, f32[1,16,256]{2,1,0:T(8,128)} %storage_ref.1, f32[1,16,256]{2,1,0:T(8,128)} %kappa_ref.1, f32[1,16,256,256]{3,2,1,0:T(8,128)} %inverse_hbm.1, s32[1,16,256]{2,1,0:T(8,128)} %mask_ref.1, ...), custom_call_target="tpu_custom_call" | custom-call | tf_op jit(solution)/shard_map/pallas_call | solution.py:191
  33.4 1.3 %fusion = (f32[1,16,256]{2,1,0:T(8,128)}, f32[1,16,256]{2,1,0:T(8,128)}) fusion(f32[2,16,256]{2,1,0:T(8,128)} %shard_map.95), kind=kLoop, calls=%fused_computation | loop fusion | bytes 65536 | tf_op jit(solution)/shard_map/slice | solution.py:216

commit v3 on v2

--- a/solution.py
+++ b/solution.py
@@ -116,7 +116,8 @@
         links = jnp.where(row == chain, upstream_ref[0, chain], links)
     live = mask_ref[0].astype(jnp.float32)
     rates = kappa_ref[0]
-    picked = [row == chain for chain in range(rows)]
+    half = rows // 2
+    picked = [lax.rem(iota((2 * half, width), 0), half) == chain for chain in range(half)]
 
     runoff = own
     for at, copy in enumerate(sends):
@@ -125,15 +126,19 @@
     forcing = time_step * runoff
 
     def product(vector):
-        head, tail = two_terms(vector)
-        total = jnp.zeros((2 * rows, width), jnp.float32)
-        zero = jnp.zeros_like(head)
-        for chain in range(rows):
-            upper = jnp.where(picked[chain], head, zero)
-            left = jnp.concatenate([upper, jnp.where(picked[chain], tail, zero)], axis=0)
-            total += jnp.dot(left, heads[chain], preferred_element_type=jnp.float32)
-            total += jnp.dot(left, tails[chain], preferred_element_type=jnp.float32)
-        return total[:rows] + total[rows:]
+        head = vector.astype(jnp.bfloat16).astype(jnp.float32)
+        tail = vector - head
+        starts = range(0, rows, half)
+        lefts = [jnp.concatenate([head[start:start + half], tail[start:start + half]], axis=0).astype(jnp.bfloat16) for start in starts]
+        totals = [jnp.zeros((2 * half, width), jnp.float32) for _ in starts]
+        for chain in range(half):
+            for at, start in enumerate(starts):
+                single = jnp.where(picked[chain], lefts[at], jnp.zeros_like(lefts[at]))
+                totals[at] += jnp.dot(single, heads[start + chain], preferred_element_type=jnp.float32)
+            for at, start in enumerate(starts):
+                single = jnp.where(picked[chain], lefts[at], jnp.zeros_like(lefts[at]))
+                totals[at] += jnp.dot(single, tails[start + chain], preferred_element_type=jnp.float32)
+        return jnp.concatenate([total[:half] + total[half:] for total in totals], axis=0)
 
     @pl.when(here == 0)
     def _():

time: 35.1 us -> 29.8 us (0.85)
  Pallas kernels: 32.8 us -> 27.6 us
    pallas_call x1, Pallas kernels: 32.8 us -> 27.6 us  [local(): pl.pallas_call(functools.partial(kernel, npos, nset), out_shape=jax.Shape...]
where the time goes in v3:
time: 29.8 us; the launch traced here: 29.5 us
  Pallas kernels  27.6 us (93%)
  local copies, waits for them, and re-layouts  1.35 us (5%)
  between operations  0.64 us (2%)
    pallas_call x1, Pallas kernels, local(): pl.pallas_call(functools.partial(kernel, npos, nset), out_shape=jax.Shape...  27.6 us
    slice x1, local copies, waits for them, and re-layouts, local(): return (out[:1], out[1:])  1.35 us

profile of v3, /device:TPU:7, one launch (start us, length us, event | category | flops | bytes accessed | tf_op | source)
XLA Modules:
  0.0 29.5 jit_solution(12827276639828382890)
XLA Ops:
  0.6 27.6 %shard_map.95 = f32[2,16,256]{2,1,0:T(8,128)} custom-call(f32[1,64,1024]{2,1,0:T(8,128)} %water_hbm.1, f32[1,64,1024]{2,1,0:T(8,128)} %frac_hbm.1, s32[1,64,1024]{2,1,0:T(8,128)} %cell_hbm.1, f32[1,16,256]{2,1,0:T(8,128)} %storage_ref.1, f32[1,16,256]{2,1,0:T(8,128)} %kappa_ref.1, f32[1,16,256,256]{3,2,1,0:T(8,128)} %inverse_hbm.1, s32[1,16,256]{2,1,0:T(8,128)} %mask_ref.1, ...), custom_call_target="tpu_custom_call" | custom-call | tf_op jit(solution)/shard_map/pallas_call | solution.py:196
  28.2 1.3 %fusion = (f32[1,16,256]{2,1,0:T(8,128)}, f32[1,16,256]{2,1,0:T(8,128)}) fusion(f32[2,16,256]{2,1,0:T(8,128)} %shard_map.95), kind=kLoop, calls=%fused_computation | loop fusion | bytes 65536 | tf_op jit(solution)/shard_map/slice | solution.py:221

commit v4 on v3

--- a/solution.py
+++ b/solution.py
@@ -22,10 +22,10 @@
     return lax.broadcasted_iota(jnp.int32, shape, axis)
 
 
-def kernel(npos, nset, water_hbm, frac_hbm, cell_hbm, storage_ref, kappa_ref, inverse_hbm, mask_ref, upstream_ref,
+def kernel(npos, nset, water_hbm, frac_hbm, cell_hbm, storage_hbm, kappa_hbm, inverse_hbm, mask_hbm, upstream_hbm,
            out_ref,
-           water, frac, cell, inverse, heads, tails, part, arrived, flow, inflow,
-           tile_sem, inverse_sem, part_send, part_recv, flow_send, flow_recv):
+           storage_ref, kappa_ref, mask_ref, upstream_ref, water, frac, cell, inverse, heads, tails, part, arrived, flow, inflow,
+           small_sem, tile_sem, inverse_sem, part_send, part_recv, flow_send, flow_recv):
     rows, width = storage_ref.shape[1], storage_ref.shape[2]
     low = 1 << (width.bit_length() // 2)
     high = width // low
@@ -55,6 +55,11 @@
             copy.start()
             group.append(copy)
         loads.append(group)
+    small_loads = []
+    for at, (source, target) in enumerate(((storage_hbm, storage_ref), (kappa_hbm, kappa_ref), (mask_hbm, mask_ref), (upstream_hbm, upstream_ref))):
+        copy = pltpu.make_async_copy(source, target, small_sem.at[at])
+        copy.start()
+        small_loads.append(copy)
     matrix_loads = []
     for chain in range(rows):
         copy = pltpu.make_async_copy(inverse_hbm.at[0, chain], inverse.at[chain], inverse_sem.at[chain])
@@ -110,6 +115,8 @@
         heads[chain] = head
         tails[chain] = tail
 
+    for copy in small_loads:
+        copy.wait()
     row = iota((rows, width), 0)
     links = jnp.zeros((rows, width), jnp.int32)
     for chain in range(rows):
@@ -192,13 +199,16 @@
         tiles = tile_water.shape[2]
         anywhere = pl.BlockSpec(memory_space=pl.ANY)
         vmem = pl.BlockSpec(memory_space=pltpu.VMEM)
-        smem = pl.BlockSpec(memory_space=pltpu.SMEM)
         out = pl.pallas_call(
             functools.partial(kernel, npos, nset),
             out_shape=jax.ShapeDtypeStruct((2, rows, width), jnp.float32),
-            in_specs=[anywhere, anywhere, anywhere, vmem, vmem, anywhere, vmem, smem],
+            in_specs=[anywhere] * 8,
             out_specs=vmem,
             scratch_shapes=[
+                pltpu.VMEM(storage.shape, jnp.float32),
+                pltpu.VMEM(kappa.shape, jnp.float32),
+                pltpu.VMEM(cell_mask.shape, jnp.int32),
+                pltpu.SMEM(upstream.shape, jnp.int32),
                 pltpu.VMEM((nset, rows, tiles), jnp.float32),
                 pltpu.VMEM((nset, rows, tiles), jnp.float32),
                 pltpu.VMEM((nset, rows, tiles), jnp.int32),
@@ -209,6 +219,7 @@
                 pltpu.VMEM((nset - 1, rows, width), jnp.float32),
                 pltpu.VMEM((SUBSTEPS, rows, width), jnp.float32),
                 pltpu.VMEM((SUBSTEPS, rows, width), jnp.float32),
+                pltpu.SemaphoreType.DMA((4,)),
                 pltpu.SemaphoreType.DMA((nset, 3)),
                 pltpu.SemaphoreType.DMA((rows,)),
                 pltpu.SemaphoreType.DMA((nset - 1,)),

time: 29.8 us -> 29.1 us (0.977)
  Pallas kernels: 27.6 us -> 26.8 us
    pallas_call x1, Pallas kernels: 27.6 us -> 26.8 us  [local(): pl.pallas_call(functools.partial(kernel, npos, nset), out_shape=jax.Shape...]
where the time goes in v4:
time: 29.1 us; the launch traced here: 28.8 us
  Pallas kernels  26.8 us (92%)
  local copies, waits for them, and re-layouts  1.35 us (5%)
  between operations  0.64 us (2%)
    pallas_call x1, Pallas kernels, local(): pl.pallas_call(functools.partial(kernel, npos, nset), out_shape=jax.Shape...  26.8 us
    slice x1, local copies, waits for them, and re-layouts, local(): return (out[:1], out[1:])  1.35 us

profile of v4, /device:TPU:7, one launch (start us, length us, event | category | flops | bytes accessed | tf_op | source)
XLA Modules:
  0.0 28.8 jit_solution(8795840063774789002)
XLA Ops:
  0.6 26.8 %shard_map.95 = f32[2,16,256]{2,1,0:T(8,128)} custom-call(f32[1,64,1024]{2,1,0:T(8,128)} %water_hbm.1, f32[1,64,1024]{2,1,0:T(8,128)} %frac_hbm.1, s32[1,64,1024]{2,1,0:T(8,128)} %cell_hbm.1, f32[1,16,256]{2,1,0:T(8,128)} %storage_hbm.1, f32[1,16,256]{2,1,0:T(8,128)} %kappa_hbm.1, f32[1,16,256,256]{3,2,1,0:T(8,128)} %inverse_hbm.1, s32[1,16,256]{2,1,0:T(8,128)} %mask_hbm.1, ...), custom_call_target="tpu_custom_call" | custom-call | tf_op jit(solution)/shard_map/pallas_call | solution.py:202
  27.5 1.3 %fusion = (f32[1,16,256]{2,1,0:T(8,128)}, f32[1,16,256]{2,1,0:T(8,128)}) fusion(f32[2,16,256]{2,1,0:T(8,128)} %shard_map.95), kind=kLoop, calls=%fused_computation | loop fusion | bytes 65536 | tf_op jit(solution)/shard_map/slice | solution.py:232

commit v5 on v4

--- a/solution.py
+++ b/solution.py
@@ -95,10 +95,16 @@
     for order, step in enumerate(steps):
         for copy in loads[order]:
             copy.wait()
+        if step == 0:
+            for copy in matrix_loads + small_loads:
+                copy.wait()
+            own = cell_sums(order)
+            for chain in range(rows):
+                head, tail = two_terms(inverse[chain].T)
+                heads[chain] = head
+                tails[chain] = tail
+            continue
         sums = cell_sums(order)
-        if step == 0:
-            own = sums
-            continue
         part[step - 1] = sums
         if order == 0:
             pl.semaphore_wait(barrier, nset - 1 + jnp.minimum(here, 1) + jnp.minimum(npos - 1 - here, 1))
@@ -109,14 +115,6 @@
         copy.start()
         sends.append(copy)
 
-    for chain in range(rows):
-        matrix_loads[chain].wait()
-        head, tail = two_terms(inverse[chain].T)
-        heads[chain] = head
-        tails[chain] = tail
-
-    for copy in small_loads:
-        copy.wait()
     row = iota((rows, width), 0)
     links = jnp.zeros((rows, width), jnp.int32)
     for chain in range(rows):

time: 29.1 us -> 28.4 us (0.976)
  Pallas kernels: 26.8 us -> 26.2 us
    pallas_call x1, Pallas kernels: 26.8 us -> 26.2 us  [local(): pl.pallas_call(functools.partial(kernel, npos, nset), out_shape=jax.Shape...]
where the time goes in v5:
time: 28.4 us; the launch traced here: 28.1 us
  Pallas kernels  26.2 us (92%)
  local copies, waits for them, and re-layouts  1.35 us (5%)
  between operations  0.64 us (2%)
    pallas_call x1, Pallas kernels, local(): pl.pallas_call(functools.partial(kernel, npos, nset), out_shape=jax.Shape...  26.2 us
    slice x1, local copies, waits for them, and re-layouts, local(): return (out[:1], out[1:])  1.35 us

profile of v5, /device:TPU:7, one launch (start us, length us, event | category | flops | bytes accessed | tf_op | source)
XLA Modules:
  0.0 28.1 jit_solution(2837307790574582772)
XLA Ops:
  0.6 26.2 %shard_map.95 = f32[2,16,256]{2,1,0:T(8,128)} custom-call(f32[1,64,1024]{2,1,0:T(8,128)} %water_hbm.1, f32[1,64,1024]{2,1,0:T(8,128)} %frac_hbm.1, s32[1,64,1024]{2,1,0:T(8,128)} %cell_hbm.1, f32[1,16,256]{2,1,0:T(8,128)} %storage_hbm.1, f32[1,16,256]{2,1,0:T(8,128)} %kappa_hbm.1, f32[1,16,256,256]{3,2,1,0:T(8,128)} %inverse_hbm.1, s32[1,16,256]{2,1,0:T(8,128)} %mask_hbm.1, ...), custom_call_target="tpu_custom_call" | custom-call | tf_op jit(solution)/shard_map/pallas_call | solution.py:200
  26.8 1.3 %fusion = (f32[1,16,256]{2,1,0:T(8,128)}, f32[1,16,256]{2,1,0:T(8,128)}) fusion(f32[2,16,256]{2,1,0:T(8,128)} %shard_map.95), kind=kLoop, calls=%fused_computation | loop fusion | bytes 65536 | tf_op jit(solution)/shard_map/slice | solution.py:230

commit v6 on v4

--- a/solution.py
+++ b/solution.py
@@ -95,7 +95,14 @@
     for order, step in enumerate(steps):
         for copy in loads[order]:
             copy.wait()
+        share = range(order * rows // nset, (order + 1) * rows // nset)
+        for chain in share:
+            matrix_loads[chain].wait()
         sums = cell_sums(order)
+        for chain in share:
+            head, tail = two_terms(inverse[chain].T)
+            heads[chain] = head
+            tails[chain] = tail
         if step == 0:
             own = sums
             continue
@@ -108,12 +115,6 @@
             device_id={"tile": lax.rem(mine + step, nset)}, device_id_type=MESH)
         copy.start()
         sends.append(copy)
-
-    for chain in range(rows):
-        matrix_loads[chain].wait()
-        head, tail = two_terms(inverse[chain].T)
-        heads[chain] = head
-        tails[chain] = tail
 
     for copy in small_loads:
         copy.wait()

time: 29.1 us -> 28.4 us (0.976)
  Pallas kernels: 26.8 us -> 26.2 us
    pallas_call x1, Pallas kernels: 26.8 us -> 26.2 us  [local(): pl.pallas_call(functools.partial(kernel, npos, nset), out_shape=jax.Shape...]
where the time goes in v6:
time: 28.4 us; the launch traced here: 28.2 us
  Pallas kernels  26.2 us (92%)
  local copies, waits for them, and re-layouts  1.35 us (5%)
  between operations  0.64 us (2%)
    pallas_call x1, Pallas kernels, local(): pl.pallas_call(functools.partial(kernel, npos, nset), out_shape=jax.Shape...  26.2 us
    slice x1, local copies, waits for them, and re-layouts, local(): return (out[:1], out[1:])  1.35 us

profile of v6, /device:TPU:7, one launch (start us, length us, event | category | flops | bytes accessed | tf_op | source)
XLA Modules:
  0.0 28.2 jit_solution(10446543553478511691)
XLA Ops:
  0.6 26.2 %shard_map.95 = f32[2,16,256]{2,1,0:T(8,128)} custom-call(f32[1,64,1024]{2,1,0:T(8,128)} %water_hbm.1, f32[1,64,1024]{2,1,0:T(8,128)} %frac_hbm.1, s32[1,64,1024]{2,1,0:T(8,128)} %cell_hbm.1, f32[1,16,256]{2,1,0:T(8,128)} %storage_hbm.1, f32[1,16,256]{2,1,0:T(8,128)} %kappa_hbm.1, f32[1,16,256,256]{3,2,1,0:T(8,128)} %inverse_hbm.1, s32[1,16,256]{2,1,0:T(8,128)} %mask_hbm.1, ...), custom_call_target="tpu_custom_call" | custom-call | tf_op jit(solution)/shard_map/pallas_call | solution.py:203
  26.8 1.3 %fusion = (f32[1,16,256]{2,1,0:T(8,128)}, f32[1,16,256]{2,1,0:T(8,128)}) fusion(f32[2,16,256]{2,1,0:T(8,128)} %shard_map.95), kind=kLoop, calls=%fused_computation | loop fusion | bytes 65536 | tf_op jit(solution)/shard_map/slice | solution.py:233
